TPU v7x, 128 devices: a whole 4x4x4 slice. The times are simulated.
128 devices in a mesh: row: 8 (over z_hi, y), col: 16 (over x, z_lo, core).
Axes of the slice: x: 4, y: 4, z: 4 (z_hi: 2, z_lo: 2; z = z_hi * 2 + z_lo), core: 2. Of those that a mesh axis runs over, the one named last changes fastest.
Arguments:
- sim: bfloat16 [16384, 16384], P('row', 'col'), may hold values from -6 to 6
- diag_blocks: bfloat16 [2048, 16384], P(None, 'col'), may hold values from -0.125 to 0.125
- match_perm: int32 [8, 2048], replicated, may hold values from 0 to 2047, each once within a row
- match_scale: float32 [8, 2048], replicated, may hold values from 0.3 to 1.5
- features: bfloat16 [16384, 256], P('col'), may hold values from -0.046875 to 0.046875
Outputs:
- new_sim: bfloat16 [16384, 16384], P('row', 'col')
- aggregated: float32 [16384, 256], P(('row', 'col'))
Inputs may be any that keep to these rules, and one draw needn't show every extreme that they name: Each row of match_perm lists every number of 0 to 2047 once.
All inputs are finite; a program needn't handle non-finite values.
Results may differ from a plain program's by a relative error of at most 0.0058.
Values may be sent and summed in bfloat16 or wider, within the bound.
A program may use at most 128 MiB of HBM per device.

v0:
```python
import jax
import jax.numpy as jnp
from jax import lax
from jax.sharding import PartitionSpec as P

decay_factor = 0.8


def partner_2(value, axis, bit):
    mask = 2**bit
    pairs = [(source, source ^ mask) for source in range(lax.axis_size(axis))]
    return lax.ppermute(value, axis, pairs)


def shifted(value, axis, steps):
    count = lax.axis_size(axis)
    pairs = [(source, (source + steps) % count) for source in range(count)]
    return lax.ppermute(value, axis, pairs)


def rows_for(lines, size):
    spare = -lines.shape[0] % size
    if not spare:
        return lines
    return jnp.concatenate([lines, jnp.zeros((spare, *lines.shape[1:]), lines.dtype)])


def broadcast_by_parts(x, axis, root):
    lines = jnp.where(lax.axis_index(axis) == root, x, jnp.zeros_like(x)).reshape(
        -1, *x.shape[1:][-1:]
    )
    padded = rows_for(lines, lax.axis_size(axis))
    own = lax.psum_scatter(padded, axis, scatter_dimension=0, tiled=True)
    return lax.all_gather(own, axis, axis=0, tiled=True)[: len(lines)].reshape(x.shape)


def split_up(x, dim, size):
    dims = x.shape
    parts = x.reshape(*dims[:dim], size, dims[dim] // size, *dims[dim + 1 :])
    return jnp.moveaxis(parts, dim, 0)


def sum_at_owner(x, axis, dim):
    size = lax.axis_size(axis)
    parts = lax.all_to_all(split_up(x, dim, size), axis, 0, 0, tiled=True)
    return jnp.sum(parts, axis=0)


def on_device(sim, diag_blocks, match_perm, match_scale, features):
    row_count = lax.axis_size("row")
    col_count = lax.axis_size("col")
    blocks_here = col_count // 2 // row_count
    row_id = lax.axis_index("row")
    col_id = lax.axis_index("col")
    block_id = col_id // 2
    side = col_id % 2
    half_width = sim.shape[1]
    tile_rows = sim.shape[0]
    partner = partner_2(sim, "col", 0)
    first_half = jnp.where(side == 0, sim, partner)
    second_half = jnp.where(side == 0, partner, sim)
    whole_block = jnp.concatenate([first_half, second_half], axis=1)
    perm_block = lax.dynamic_index_in_dim(match_perm, block_id, 0, keepdims=False)
    scale_block = lax.dynamic_index_in_dim(match_scale, block_id, 0, keepdims=False)
    own_perm = lax.dynamic_slice_in_dim(perm_block, side * half_width, half_width, 0)
    own_scale = lax.dynamic_slice_in_dim(scale_block, side * half_width, half_width, 0)
    moved_cols = (jnp.take(whole_block, own_perm, axis=1) * own_scale[None, :]).astype(jnp.bfloat16)
    arrived_cols = shifted(moved_cols, "col", col_count // 2)
    mixed = (
        jnp.dot(whole_block, diag_blocks, preferred_element_type=jnp.float32) + arrived_cols
    ).astype(jnp.bfloat16)
    position = 0
    source = row_id * blocks_here + position
    perm_rows = lax.dynamic_index_in_dim(match_perm, source, 0, keepdims=False)
    scale_rows = lax.dynamic_index_in_dim(match_scale, source, 0, keepdims=False)
    sent_rows = (jnp.take(mixed, perm_rows, axis=0) * scale_rows[:, None]).astype(jnp.bfloat16)
    arrived_rows = shifted(sent_rows, "row", row_count // 2)
    position = 0
    target = row_id * blocks_here + position
    halves = []
    for part in range(2):
        left_half = broadcast_by_parts(diag_blocks, "col", 2 * target + part)
        halves.append(
            lax.dot_general(
                left_half, mixed, (((0,), (0,)), ((), ())), preferred_element_type=jnp.float32
            )
        )
    product = jnp.concatenate(halves, axis=0)
    results = decay_factor * (product + arrived_rows)
    global_rows = row_id * tile_rows + lax.broadcasted_iota(jnp.int32, results.shape, 0)
    global_cols = col_id * half_width + lax.broadcasted_iota(jnp.int32, results.shape, 1)
    new_sim = jnp.where(global_rows == global_cols, 1.0, results).astype(jnp.bfloat16)
    partial_value = jnp.dot(new_sim, features, preferred_element_type=jnp.float32)
    aggregated = sum_at_owner(partial_value, "col", 0)
    return (new_sim, aggregated)


def solution(mesh):
    placed = (P("row", "col"), P(None, "col"), P(), P(), P("col", None))
    return jax.shard_map(
        on_device,
        mesh=mesh,
        in_specs=placed,
        out_specs=(P("row", "col"), P(("row", "col"), None)),
        check_vma=False,
    )
```

profile of v0, /device:TPU:39, one launch (start us, length us, event | category | flops | bytes accessed | tf_op | source)
XLA Modules:
  0.0 421.7 jit_solution(9150470076904124508)
XLA Ops:
  7.2 0.0 copy-start
  7.2 0.0 reduce-scatter.3.cloned.1.call-start
  7.2 6.1 %broadcast_select_fusion.3 = (bf16[2048,1024]{1,0:T(8,128)(2,1)}, bf16[2048,1024]{1,0:T(8,128)(2,1)}) fusion(bf16[2048,1024]{1,0:T(8,128)(2,1)} %param.6, pred[]{:T(512)S(6)} %eq.16, pred[]{:T(512)S(6)} %eq.18), kind=kLoop, calls=%fused_computation.14 | loop fusion | flops 4194304 | bytes 12582914 | tf_op jit(solution)/shard_map/jit(_where)/select_n | solution.py:29
  13.3 0.0 reduce-scatter.3.cloned.1.call-update
  13.3 0.0 reduce-scatter.5.cloned.1.call-start
  13.4 0.7 reduce-scatter.5.cloned.1.call-update
  14.1 0.0 all-gather.3.cloned.1.call-start
  14.1 6.5 %copy.12 = bf16[2048,1024]{0,1:T(8,128)(2,1)} copy(bf16[2048,1024]{1,0:T(8,128)(2,1)} %param.5) | data formatting | bytes 8388608 | tf_op args[0]
  20.7 0.7 collective-permute-start
  21.4 61.1 %reduce-scatter.3.cloned.1.call-done = bf16[128,1024]{1,0:T(8,128)(2,1)} async-done(((bf16[2048,1024]{1,0:T(8,128)(2,1)}), bf16[128,1024]{1,0:T(8,128)(2,1)}) %reduce-scatter.3.cloned.1.call-update) | async-done | bytes 262160 | tf_op jit(solution)/shard_map/reduce_scatter | solution.py:33
  82.4 0.0 all-gather.3.cloned.1.call-update
  82.5 0.0 all-gather.5.cloned.1.call-start
  82.5 0.8 dynamic_slice.23
  83.4 0.8 compare_select_fusion.1
  84.2 0.0 collective-permute-done
  84.3 5.9 %broadcast_select_fusion.2 = (bf16[2048,1024]{0,1:T(8,128)(2,1)}, bf16[2048,1024]{0,1:T(8,128)(2,1)}) fusion(bf16[2048,1024]{0,1:T(8,128)(2,1)} %copy.12, bf16[2048,1024]{0,1:T(8,128)(2,1)} %collective-permute-done, pred[]{:T(512)S(6)} %eq.17), kind=kLoop, calls=%fused_computation.13 | loop fusion | flops 4194304 | bytes 16777216 | tf_op jit(solution)/shard_map/jit(_where)/select_n | solution.py:60
  90.1 8.4 %pad_maximum_fusion = bf16[2048,2048]{0,1:T(8,128)(2,1)} fusion(bf16[2048,1024]{0,1:T(8,128)(2,1)} %get-tuple-element.7, bf16[2048,1024]{0,1:T(8,128)(2,1)} %get-tuple-element.6), kind=kLoop, calls=%fused_computation.2 | loop fusion | flops 16777216 | bytes 16777216 | tf_op jit(solution)/shard_map/concatenate | solution.py:62
  98.5 13.3 %gather_fusion = bf16[1024,2048]{1,0:T(8,128)(2,1)} fusion(bf16[2048,2048]{0,1:T(8,128)(2,1)} %pad_maximum_fusion, s32[1024]{0:T(1024)S(1)} %broadcast_clamp_fusion.1), kind=kCustom, calls=%fused_computation | custom fusion | bytes 8392704 | tf_op jit(solution)/shard_map/jit(_take)/gather | solution.py:67
  111.7 6.4 %copy.14 = bf16[1024,2048]{0,1:T(8,128)(2,1)} copy(bf16[1024,2048]{1,0:T(8,128)(2,1)} %gather_fusion) | data formatting | bytes 8388608 | tf_op jit(solution)/shard_map/jit(_take)/gather | solution.py:67
  118.2 5.4 %fusion.3 = bf16[2048,1024]{1,0:T(8,128)(2,1)} fusion(f32[1024]{0:T(1024)S(1)} %bitcast.24, bf16[1024,2048]{0,1:T(8,128)(2,1)} %copy.14, pred[1024]{0:T(1024)(128)(4,1)S(1)} %compare_and_fusion.1), kind=kLoop, calls=%fused_computation.10 | loop fusion | flops 8388608 | bytes 8393728 | tf_op jit(solution)/shard_map/convert_element_type | solution.py:67
  123.6 0.0 collective-permute-start.1
  123.6 104.9 %reduce-scatter.5.cloned.1.call-done = bf16[128,1024]{1,0:T(8,128)(2,1)} async-done(((bf16[2048,1024]{1,0:T(8,128)(2,1)}), bf16[128,1024]{1,0:T(8,128)(2,1)}) %reduce-scatter.5.cloned.1.call-update) | async-done | bytes 262160 | tf_op jit(solution)/shard_map/reduce_scatter | solution.py:33
  228.5 0.0 all-gather.5.cloned.1.call-update
  228.5 0.9 constant_dynamic-slice_fusion
  229.4 0.9 compare_select_fusion
  230.3 0.0 collective-permute-done.1
  230.3 14.6 %add_convert_fusion = bf16[2048,1024]{1,0:T(8,128)(2,1)} fusion(bf16[2048,1024]{1,0:T(8,128)(2,1)} %collective-permute-done.1, bf16[2048,1024]{1,0:T(8,128)(2,1)} %param.6, bf16[2048,1024]{0,1:T(8,128)(2,1)} %get-tuple-element.7, bf16[2048,1024]{0,1:T(8,128)(2,1)} %get-tuple-element.6), kind=kOutput, calls=%fused_computation.9 | convolution fusion | flops 8613003264 | bytes 20971520 | tf_op jit(solution)/shard_map/dot_general | solution.py:70
  244.9 13.7 %gather_fusion.1 = bf16[2048,1024]{1,0:T(8,128)(2,1)} fusion(bf16[2048,1024]{1,0:T(8,128)(2,1)} %add_convert_fusion, s32[2048]{0:T(1024)S(1)} %broadcast_clamp_fusion), kind=kCustom, calls=%fused_computation.1 | custom fusion | bytes 8396800 | tf_op jit(solution)/shard_map/jit(_take)/gather | solution.py:76
  258.6 4.2 multiply_convert_fusion.1
  262.8 4.2 %collective-permute-start.2 = (bf16[2048,1024]{1,0:T(8,128)(2,1)}, bf16[2048,1024]{1,0:T(8,128)(2,1)}, u32[]{:S(2)}, u32[]{:S(2)}) collective-permute-start(bf16[2048,1024]{1,0:T(8,128)(2,1)} %multiply_convert_fusion.1), channel_id=1, source_target_pairs={{0,64},{16,80},{32,96},{48,112},{64,0},{80,16},{96,32},{112,48},{1... | collective-permute-start | bytes 12582920 | tf_op jit(solution)/shard_map/ppermute | solution.py:18
  267.0 5.1 %all-gather.3.cloned.1.call-done = bf16[2048,1024]{1,0:T(8,128)(2,1)} async-done(((bf16[128,1024]{1,0:T(8,128)(2,1)}), bf16[2048,1024]{1,0:T(8,128)(2,1)}) %all-gather.3.cloned.1.call-update) | async-done | bytes 4194320 | tf_op jit(solution)/shard_map/all_gather | solution.py:34
  272.2 10.0 %fusion.4 = f32[1024,1024]{1,0:T(8,128)} fusion(bf16[2048,1024]{1,0:T(8,128)(2,1)} %all-gather.3.cloned.1.call-done, bf16[2048,1024]{1,0:T(8,128)(2,1)} %add_convert_fusion), kind=kOutput, calls=%fused_computation.27 | convolution fusion | flops 4294967296 | bytes 12582912 | tf_op jit(solution)/shard_map/dot_general | solution.py:84
  282.2 47.1 %all-gather.5.cloned.1.call-done = bf16[2048,1024]{1,0:T(8,128)(2,1)} async-done(((bf16[128,1024]{1,0:T(8,128)(2,1)}), bf16[2048,1024]{1,0:T(8,128)(2,1)}) %all-gather.5.cloned.1.call-update) | async-done | bytes 4194320 | tf_op jit(solution)/shard_map/all_gather | solution.py:34
  329.3 0.0 copy-start.2
  329.3 7.7 %fusion.5 = f32[1024,1024]{1,0:T(8,128)S(1)} fusion(bf16[2048,1024]{1,0:T(8,128)(2,1)} %all-gather.5.cloned.1.call-done, bf16[2048,1024]{1,0:T(8,128)(2,1)} %add_convert_fusion), kind=kOutput, calls=%fused_computation.28 | convolution fusion | flops 4294967296 | bytes 12582912 | tf_op jit(solution)/shard_map/dot_general | solution.py:84
  337.0 40.3 %collective-permute-done.2 = bf16[2048,1024]{1,0:T(8,128)(2,1)} collective-permute-done((bf16[2048,1024]{1,0:T(8,128)(2,1)}, bf16[2048,1024]{1,0:T(8,128)(2,1)}, u32[]{:S(2)}, u32[]{:S(2)}) %collective-permute-start.2) | collective-permute-done | bytes 4194336 | tf_op jit(solution)/shard_map/ppermute | solution.py:18
  377.3 0.0 copy-done.2
  377.3 4.1 fusion.2
  381.4 0.0 copy-done
  381.4 0.0 copy-start.1
  381.4 1.3 fusion.6
  382.7 0.7 copy-done.1
  383.4 31.0 %all_to_all.5 = f32[16,128,256]{2,1,0:T(8,128)S(1)} all-to-all(f32[16,128,256]{2,1,0:T(8,128)S(1)} %bitcast.20), channel_id=1, replica_groups=mesh['row'=8,'col'=16] {'col'}, dimensions={0} | all-to-all | bytes 4194304 | tf_op jit(solution)/shard_map/all_to_all | solution.py:45
  414.4 0.8 reduce_sum.9
  (6 shorter events, 0.0 us)
Async XLA Ops:
  7.2 374.2 %copy-start = (bf16[1024,256]{1,0:T(8,128)(2,1)S(1)}, bf16[1024,256]{1,0:T(8,128)(2,1)}, u32[]{:S(2)}) copy-start(bf16[1024,256]{1,0:T(8,128)(2,1)} %param.9) | copy-start | bytes 1572868
  7.2 75.3 %reduce-scatter.3.cloned.1.call-start = ((), (), s32[]{:S(2)}) async-start(), calls=%async_computation.3 | async-start | bytes 4456448 | tf_op jit(solution)/shard_map/reduce_scatter | solution.py:33
  13.3 215.2 %reduce-scatter.5.cloned.1.call-start = ((), (), s32[]{:S(2)}) async-start(), calls=%async_computation.5 | async-start | bytes 4456448 | tf_op jit(solution)/shard_map/reduce_scatter | solution.py:33
  14.1 258.1 %all-gather.3.cloned.1.call-start = ((), (), s32[]{:S(2)}) async-start(), calls=%async_computation.4 | async-start | bytes 4456448 | tf_op jit(solution)/shard_map/all_gather | solution.py:34
  20.7 63.6 %collective-permute-start = (bf16[2048,1024]{0,1:T(8,128)(2,1)}, bf16[2048,1024]{0,1:T(8,128)(2,1)}, u32[]{:S(2)}, u32[]{:S(2)}) collective-permute-start(bf16[2048,1024]{0,1:T(8,128)(2,1)} %copy.12), channel_id=1, source_target_pairs={{0,1},{1,0},{2,3},{3,2},{4,5},{5,4},{6,7},{7,6},{8,9},{9,8},{10,11... | collective-permute-start | bytes 12582920 | tf_op jit(solution)/shard_map/ppermute | solution.py:12
  82.5 246.8 %all-gather.5.cloned.1.call-start = ((), (), s32[]{:S(2)}) async-start(), calls=%async_computation.6 | async-start | bytes 4456448 | tf_op jit(solution)/shard_map/all_gather | solution.py:34
  123.6 106.7 %collective-permute-start.1 = (bf16[2048,1024]{1,0:T(8,128)(2,1)}, bf16[2048,1024]{1,0:T(8,128)(2,1)}, u32[]{:S(2)}, u32[]{:S(2)}) collective-permute-start(bf16[2048,1024]{1,0:T(8,128)(2,1)} %fusion.3), channel_id=1, source_target_pairs={{0,8},{1,9},{2,10},{3,11},{4,12},{5,13},{6,14},{7,15},{8,0},{9,1},... | collective-permute-start | bytes 12582920 | tf_op jit(solution)/shard_map/ppermute | solution.py:18
  262.8 114.5 %collective-permute-start.2 = (bf16[2048,1024]{1,0:T(8,128)(2,1)}, bf16[2048,1024]{1,0:T(8,128)(2,1)}, u32[]{:S(2)}, u32[]{:S(2)}) collective-permute-start(bf16[2048,1024]{1,0:T(8,128)(2,1)} %multiply_convert_fusion.1), channel_id=1, source_target_pairs={{0,64},{16,80},{32,96},{48,112},{64,0},{80,16},{96,32},{112,48},{1... | collective-permute-start | bytes 12582920 | tf_op jit(solution)/shard_map/ppermute | solution.py:18
  329.3 48.0 %copy-start.2 = (f32[1024,1024]{1,0:T(8,128)S(1)}, f32[1024,1024]{1,0:T(8,128)}, u32[]{:S(2)}) copy-start(f32[1024,1024]{1,0:T(8,128)} %fusion.4) | copy-start | bytes 12582916
  381.4 2.0 copy-start.1
Sparse Core Ops, SparseCore 0:
  13.5 68.9 reduce-scatter.2
  84.8 143.6 reduce-scatter.4
  230.2 41.9 all-gather.2
  273.7 55.5 all-gather.4
where the time goes:
time: 426 us; the launch traced here: 422 us
  waiting for transfers between devices  259 us (61%)
  local copies, waits for them, and re-layouts  42.4 us (10%)
  other arithmetic  36.5 us (9%)
  matrix products  33.7 us (8%)
  blocking collectives  31 us (7%)
  between operations  13.9 us (3%)
  starting transfers between devices  5.05 us (1%)
    reduce_scatter x2, waiting for transfers between devices, broadcast_by_parts(): own = lax.psum_scatter(padded, axis, scatter_dimension=0, tiled=True)  166 us
    all_gather x2, waiting for transfers between devices, broadcast_by_parts(): lax.all_gather(own, axis, axis=0, tiled=True)[:len(lines)].reshape(x.shape)  52.2 us
    ppermute x2, waiting for transfers between devices, shifted(): return lax.ppermute(value, axis, pairs)  40.3 us
    all_to_all x1, blocking collectives, sum_at_owner(): parts = lax.all_to_all(split_up(x, dim, size), axis, 0, 0, tiled=True)  31 us
    gather x2, local copies, waits for them, and re-layouts, on_device(): jnp.take(whole_block, own_perm, axis=1) * own_scale[None, :]  19.7 us
    dot_general x2, matrix products, on_device(): lax.dot_general(left_half, mixed, (((0,), (0,)), ((), ())), preferred_ele...  17.8 us
    dot_general x1, matrix products, on_device(): jnp.dot(whole_block, diag_blocks, preferred_element_type=jnp.float32)  14.6 us
    gather x1, local copies, waits for them, and re-layouts, on_device(): jnp.take(mixed, perm_rows, axis=0) * scale_rows[:, None]  13.7 us
  transfers between devices with their start and end apart: 7, of which 5 were waited for; matrix products, arithmetic and copies ran while one was open for 24% of the time, Pallas kernels for 0%

commit v1 on v0

v1 whole, which is shorter than its diff:
```python
import jax
import jax.numpy as jnp
from jax import lax
from jax.experimental import pallas as pl
from jax.experimental.pallas import tpu as pltpu
from jax.sharding import PartitionSpec as P

decay_factor = 0.8
MESH = pl.DeviceIdType.MESH

NB = 2048
HALF = 1024
F = 256
CH = 256
NCH = NB // CH
PIECE = 128
BF16 = jnp.bfloat16
F32 = jnp.float32


def kernel(
    sim, diag, perm, scale, feat,
    new_sim, agg,
    s_own, s_par, b_own, onehot, mixed, sent, marr, bt, acc, feats,
    mine_t, perm_row, scale_row, perm_col, inv_scale, part, slots, total,
    load_sem, own_sem,
    sx, rx, sz, rz, sd, rd, sf, rf, sb, rb, se, sc, rc, sa, ra, out_sem, agg_sem,
):
    row = lax.axis_index("row")
    col = lax.axis_index("col")
    zh, y = row // 4, row % 4
    x, zl, core = col // 4, (col // 2) % 2, col % 2
    block = col // 2
    sibling = (row, col + 1 - 2 * core)
    x_partner = (row, (col + 8) % 16)
    z_partner = ((row + 4) % 8, col)
    near = (row, col + 2 - 4 * zl)
    hold_same = (x // 2 == zh).astype(jnp.int32)
    hold_piece = y + 4 * (1 - hold_same)
    hold_zl = lax.rem(zl + 1 - hold_same, 2)
    parity = y % 2
    match = (parity == zl).astype(jnp.int32)
    first = 4 * (1 - match)
    source_zh = lax.rem(zh + 1 - match, 2)

    def hold_target(i):
        return block, i * 4 + hold_zl * 2 + core

    def hold_source(i):
        return source_zh * 4 + i, (row // 2) * 4 + parity * 2 + core

    def is_me(device):
        return jnp.logical_and(device[0] == row, device[1] == col)

    barrier = pltpu.get_barrier_semaphore()

    def greet(device):
        pl.semaphore_signal(barrier, inc=1, device_id=device, device_id_type=MESH)

    for i in range(1, 16):
        greet((row, (col + i) % 16))
    greet(z_partner)
    own_source = jnp.int32(0)
    for i in range(4):
        device = hold_source(i)

        @pl.when(jnp.logical_not(is_me(device)))
        def _():
            greet(device)

    out_count = jnp.int32(16)
    for i in range(4):
        out_count = out_count + jnp.where(is_me(hold_target(i)), 0, 1)

    loads = [
        pltpu.make_async_copy(diag, b_own, load_sem.at[0]),
        pltpu.make_async_copy(feat, feats, load_sem.at[1]),
    ]
    for load in loads:
        load.start()

    def own_load(i):
        rows = pl.ds(i * CH, CH)
        return pltpu.make_async_copy(
            sim.at[rows], s_own.at[core, rows], own_sem.at[i]
        )

    for i in range(NCH):
        own_load(i).start()
    pl.semaphore_wait(barrier, out_count)

    def remote(src, dst, send, recv, device):
        return pltpu.make_async_remote_copy(
            src_ref=src, dst_ref=dst, send_sem=send, recv_sem=recv,
            device_id=device, device_id_type=MESH,
        )

    def x_copy(i):
        rows = pl.ds(i * CH, CH)
        return remote(sim.at[rows], s_par.at[core, rows], sx.at[i], rx.at[i], x_partner)

    def own_copy(i):
        rows = pl.ds(i * CH, CH)
        return remote(sim.at[rows], s_own.at[core, rows], sd.at[i], rd.at[i], sibling)

    def own_arrival(i):
        rows = pl.ds(i * CH, CH)
        return remote(sim.at[rows], s_own.at[1 - core, rows], sd.at[i], rd.at[i], sibling)

    def forward(i):
        rows = pl.ds(i * CH, CH)
        return remote(s_par.at[core, rows], s_par.at[core, rows], sf.at[i], rf.at[i], sibling)

    def forward_arrival(i):
        rows = pl.ds(i * CH, CH)
        return remote(s_par.at[core, rows], s_par.at[1 - core, rows], sf.at[i], rf.at[i], sibling)

    def z_copy(i):
        rows = pl.ds(i * CH, CH)
        return remote(sent.at[rows], marr.at[rows], sz.at[i], rz.at[i], z_partner)

    def bt_rows(half, piece):
        return pl.ds(pl.multiple_of(half * HALF + piece * PIECE, PIECE), PIECE)

    def piece_copy(i):
        device = hold_target(i)
        return remote(
            mine_t, bt.at[bt_rows(core, hold_piece)], sb.at[i], rb.at[hold_piece], device
        )

    def piece_arrival(q):
        return remote(mine_t, bt.at[bt_rows(core, q)], sb.at[0], rb.at[q], near)

    def near_copy(i):
        rows = bt_rows(core, first + i)
        return remote(bt.at[rows], bt.at[rows], se.at[i], rb.at[first + i], near)

    def core_copy(q):
        rows = bt_rows(core, q)
        return remote(bt.at[rows], bt.at[rows], sc.at[q], rc.at[q], sibling)

    def core_arrival(q):
        return remote(mine_t, bt.at[bt_rows(1 - core, q)], sc.at[q], rc.at[q], sibling)

    for i in range(2):
        x_copy(i).start()
    for i in range(NCH):
        own_copy(i).start()

    loads[0].wait()
    piece_cols = pl.ds(pl.multiple_of(hold_piece * PIECE, PIECE), PIECE)
    for i in range(NB // PIECE):
        rows = pl.ds(i * PIECE, PIECE)
        mine_t[:, rows] = b_own[rows, piece_cols].astype(F32).T.astype(BF16)
    for i in range(4):
        device = hold_target(i)
        self_copy = is_me(device)

        @pl.when(jnp.logical_not(self_copy))
        def _():
            piece_copy(i).start()

        @pl.when(self_copy)
        def _():
            pltpu.make_async_copy(
                mine_t, bt.at[bt_rows(core, hold_piece)], rb.at[hold_piece]
            ).start()

    col_source = (block + 4) % 8
    row_source = (row + 4) % 8
    lines = lax.broadcasted_iota(jnp.int32, (8, NB), 0)

    def line(table, wanted):
        return jnp.sum(jnp.where(lines == wanted, table[...], 0), axis=0, keepdims=True)

    perm_row[0:1, :] = line(perm, col_source)
    perm_row[1:2, :] = line(perm, row_source)
    perm_row[2:3, :] = line(perm, row)
    scale_row[0:1, :] = line(scale, col_source)
    scale_row[1:2, :] = line(scale, row)

    half_cols = pl.ds(pl.multiple_of(core * HALF, HALF), HALF)

    @pl.loop(0, NB // 128)
    def _(i):
        rows = pl.ds(i * 128, 128)
        wanted = perm_row[0:1, half_cols]
        here = lax.broadcasted_iota(jnp.int32, (128, HALF), 0) + i * 128
        onehot[rows, :] = jnp.where(here == wanted, 1.0, 0.0).astype(BF16)

    for i in range(NB // 128):
        part_row = perm_row[1:2, pl.ds(i * 128, 128)]
        perm_col[pl.ds(i * 128, 128), :] = jnp.broadcast_to(part_row, (128, 128)).T

    @pl.loop(0, NB // 128)
    def _(i):
        rows = pl.ds(i * 128, 128)
        here = lax.broadcasted_iota(jnp.int32, (128, NB), 0) + i * 128
        hit = jnp.where(here == perm_row[2:3, :], scale_row[1:2, :], 0.0)
        inv_scale[rows, :] = jnp.broadcast_to(jnp.sum(hit, axis=1, keepdims=True), (128, 128))

    @pl.loop(0, NCH)
    def _(i):
        rows = pl.ds(pl.multiple_of(i * CH, CH), CH)

        @pl.when(i + 2 < NCH)
        def _():
            x_copy(i + 2).start()

        x_copy(i).wait_recv()
        forward(i).start()

        @pl.when(jnp.logical_and(i >= 2, i < 6))
        def _():
            piece_arrival(first + i - 2).wait_recv()
            near_copy(i - 2).start()
            core_copy(first + i - 2).start()

        own_load(i).wait()
        own_arrival(i).wait_recv()
        forward_arrival(i).wait_recv()

        @pl.loop(0, HALF // 256)
        def _(n):
            cols = pl.ds(pl.multiple_of(n * 256, 256), 256)
            value = jnp.dot(s_own[0, rows, :], b_own[:HALF, cols], preferred_element_type=F32)
            value += jnp.dot(s_own[1, rows, :], b_own[HALF:, cols], preferred_element_type=F32)
            moved = jnp.dot(s_par[0, rows, :], onehot[:HALF, cols], preferred_element_type=F32)
            moved += jnp.dot(s_par[1, rows, :], onehot[HALF:, cols], preferred_element_type=F32)
            here = pl.ds(pl.multiple_of(core * HALF + n * 256, 256), 256)
            value += moved * scale_row[0:1, here]
            value = value.astype(BF16)
            mixed[rows, cols] = value
            lanes = inv_scale[rows, :]
            sent[rows, cols] = (
                value.astype(F32) * jnp.concatenate([lanes, lanes], axis=1)
            ).astype(BF16)

        z_copy(i).start()

    other = 4 - first

    @pl.loop(0, 4)
    def _(i):
        piece_arrival(other + i).wait_recv()
        core_copy(other + i).start()

    @pl.loop(0, 8)
    def _(q):
        core_arrival(q).wait_recv()

    @pl.loop(0, NCH)
    def _(t):
        rows = pl.ds(pl.multiple_of(t * CH, CH), CH)

        @pl.loop(0, HALF // 512)
        def _(n):
            cols = pl.ds(pl.multiple_of(n * 512, 512), 512)
            acc[rows, cols] = jnp.dot(bt[rows, :], mixed[:, cols], preferred_element_type=F32)

    def gathered(rows, i, cols):
        wanted = perm_col[rows, :]
        wanted = jnp.concatenate([wanted, wanted], axis=1)
        here = lax.broadcasted_iota(jnp.int32, (CH, CH), 1) + i * CH
        pick = jnp.where(here == wanted, 1.0, 0.0).astype(BF16)
        far = marr[pl.ds(pl.multiple_of(i * CH, CH), CH), cols]
        return jnp.dot(pick, far, preferred_element_type=F32)

    @pl.loop(0, NCH - 1)
    def _(i):
        z_copy(i).wait_recv()

        @pl.loop(0, NCH)
        def _(t):
            rows = pl.ds(pl.multiple_of(t * CH, CH), CH)
            acc[rows, :] += gathered(rows, i, pl.ds(0, HALF))

    z_copy(NCH - 1).wait_recv()
    loads[1].wait()
    offset = col * HALF - row * NB

    def out_copy(t):
        rows = pl.ds(pl.multiple_of(t * CH, CH), CH)
        return pltpu.make_async_copy(mixed.at[rows], new_sim.at[rows], out_sem.at[t])

    def part_copy(owner):
        rows = pl.ds(pl.multiple_of(owner * 128, 128), 128)
        return remote(part.at[rows], slots.at[col], sa.at[owner], ra.at[col], (row, owner))

    def part_arrival(i):
        return remote(part.at[pl.ds(0, 128)], slots.at[i], sa.at[i], ra.at[i], sibling)

    @pl.loop(0, NCH)
    def _(t):
        rows = pl.ds(pl.multiple_of(t * CH, CH), CH)
        value = decay_factor * (acc[rows, :] + gathered(rows, NCH - 1, pl.ds(0, HALF)))
        down = lax.broadcasted_iota(jnp.int32, (CH, HALF), 0) + t * CH
        across = lax.broadcasted_iota(jnp.int32, (CH, HALF), 1) + offset
        value = jnp.where(down == across, 1.0, value).astype(BF16)
        mixed[rows, :] = value
        out_copy(t).start()
        part[rows, :] = jnp.dot(value, feats[...], preferred_element_type=F32).astype(BF16)
        for k in range(2):
            owner = 2 * t + k

            @pl.when(owner != col)
            def _():
                part_copy(owner).start()

    mine = part[pl.ds(pl.multiple_of(col * 128, 128), 128), :].astype(F32)
    total[...] = mine

    @pl.loop(0, 16)
    def _(i):
        @pl.when(i != col)
        def _():
            part_arrival(i).wait_recv()
            total[...] += slots[i].astype(F32)

    agg_copy = pltpu.make_async_copy(total, agg, agg_sem)
    agg_copy.start()

    @pl.loop(0, NCH)
    def _(i):
        x_copy(i).wait_send()
        own_copy(i).wait_send()
        forward(i).wait_send()
        z_copy(i).wait_send()
        core_copy(i).wait_send()
        out_copy(i).wait()

    for i in range(4):
        near_copy(i).wait_send()

        @pl.when(jnp.logical_not(is_me(hold_target(i))))
        def _():
            piece_copy(i).wait_send()

    @pl.loop(0, 16)
    def _(i):
        @pl.when(i != col)
        def _():
            part_copy(i).wait_send()

    agg_copy.wait()


def on_device(sim, diag_blocks, match_perm, match_scale, features):
    dma = pltpu.SemaphoreType.DMA
    return pl.pallas_call(
        kernel,
        out_shape=(
            jax.ShapeDtypeStruct((NB, HALF), BF16),
            jax.ShapeDtypeStruct((128, F), F32),
        ),
        in_specs=[
            pl.BlockSpec(memory_space=pl.ANY),
            pl.BlockSpec(memory_space=pl.ANY),
            pl.BlockSpec(memory_space=pltpu.VMEM),
            pl.BlockSpec(memory_space=pltpu.VMEM),
            pl.BlockSpec(memory_space=pl.ANY),
        ],
        out_specs=(
            pl.BlockSpec(memory_space=pl.ANY),
            pl.BlockSpec(memory_space=pl.ANY),
        ),
        scratch_shapes=[
            pltpu.VMEM((2, NB, HALF), BF16),
            pltpu.VMEM((2, NB, HALF), BF16),
            pltpu.VMEM((NB, HALF), BF16),
            pltpu.VMEM((NB, HALF), BF16),
            pltpu.VMEM((NB, HALF), BF16),
            pltpu.VMEM((NB, HALF), BF16),
            pltpu.VMEM((NB, HALF), BF16),
            pltpu.VMEM((NB, NB), BF16),
            pltpu.VMEM((NB, HALF), F32),
            pltpu.VMEM((HALF, F), BF16),
            pltpu.VMEM((PIECE, NB), BF16),
            pltpu.VMEM((8, NB), jnp.int32),
            pltpu.VMEM((8, NB), F32),
            pltpu.VMEM((NB, 128), jnp.int32),
            pltpu.VMEM((NB, 128), F32),
            pltpu.VMEM((NB, F), BF16),
            pltpu.VMEM((16, 128, F), BF16),
            pltpu.VMEM((128, F), F32),
            dma((2,)), dma((NCH,)),
            dma((NCH,)), dma((NCH,)),
            dma((NCH,)), dma((NCH,)),
            dma((NCH,)), dma((NCH,)),
            dma((NCH,)), dma((NCH,)),
            dma((4,)), dma((8,)), dma((4,)),
            dma((8,)), dma((8,)),
            dma((16,)), dma((16,)),
            dma((NCH,)), dma(()),
        ],
        compiler_params=pltpu.CompilerParams(
            collective_id=0, has_side_effects=True, vmem_limit_bytes=60 * 2**20
        ),
        name="simrank",
    )(sim, diag_blocks, match_perm, match_scale, features)


def solution(mesh):
    placed = (P("row", "col"), P(None, "col"), P(), P(), P("col", None))
    return jax.shard_map(
        on_device,
        mesh=mesh,
        in_specs=placed,
        out_specs=(P("row", "col"), P(("row", "col"), None)),
        check_vma=False,
    )
```

time: 426 us -> 272 us (0.64); the launches traced: 422 us -> 272 us
  Pallas kernels: 0 us -> 266 us
  waiting for transfers between devices: 259 us -> 0 us
  local copies, waits for them, and re-layouts: 42.4 us -> 5.34 us
  other arithmetic: 36.5 us -> 0 us
  matrix products: 33.7 us -> 0 us
  blocking collectives: 31 us -> 0 us
  between operations: 13.9 us -> 0.65 us
  starting transfers between devices: 5.05 us -> 0 us
    pallas_call x0 -> x1, Pallas kernels: none -> 266 us  [on_device(): pl.pallas_call(kernel, out_shape=(jax.ShapeDtypeStruct((NB, HALF), BF16),...]
    reduce_scatter x2 -> x0, waiting for transfers between devices: 166 us -> none  [broadcast_by_parts(): own = lax.psum_scatter(padded, axis, scatter_dimension=0, tiled=True)]
    all_gather x2 -> x0, waiting for transfers between devices: 52.2 us -> none  [broadcast_by_parts(): lax.all_gather(own, axis, axis=0, tiled=True)[:len(lines)].reshape(x.shape)]
    ppermute x3 -> x0, waiting for transfers between devices: 40.3 us -> none  [the longest x2 40.3 us: shifted(): return lax.ppermute(value, axis, pairs)]
    dot_general x4 -> x0, matrix products: 33.7 us -> none  [the longest x2 17.8 us: on_device(): lax.dot_general(left_half, mixed, (((0,), (0,)), ((), ())), preferred_ele...]
    gather x3 -> x0, local copies, waits for them, and re-layouts: 33.4 us -> none  [the longest x2 19.7 us: on_device(): jnp.take(whole_block, own_perm, axis=1) * own_scale[None, :]]
    all_to_all x1 -> x0, blocking collectives: 31 us -> none  [sum_at_owner(): parts = lax.all_to_all(split_up(x, dim, size), axis, 0, 0, tiled=True)]
    convert_element_type x3 -> x0, other arithmetic: 13.7 us -> none  [the longest x1 5.42 us: on_device(): (jnp.take(whole_block, own_perm, axis=1) * own_scale[None, :]).astype(jnp...]
  transfers between devices with their start and end apart: 7 -> 0, of which waited for: 5 -> 0; matrix products, arithmetic and copies ran while one was open for 24% -> 0% of each run, Pallas kernels for 0% -> 0%
where the time goes in v1:
time: 272 us
  Pallas kernels  266 us (98%)
  local copies, waits for them, and re-layouts  5.34 us (2%)
    pallas_call x1, Pallas kernels, on_device(): pl.pallas_call(kernel, out_shape=(jax.ShapeDtypeStruct((NB, HALF), BF16),...  266 us

profile of v1, /device:TPU:39, one launch (start us, length us, event | category | flops | bytes accessed | tf_op | source)
XLA Modules:
  0.0 272.1 jit_solution(13006554565508595861)
XLA Ops:
  0.6 266.2 %simrank.1 = (bf16[2048,1024]{1,0:T(8,128)(2,1)}, f32[128,256]{1,0:T(8,128)}) custom-call(bf16[2048,1024]{1,0:T(8,128)(2,1)} %sim.1, bf16[2048,1024]{1,0:T(8,128)(2,1)} %diag.1, s32[8,2048]{1,0:T(8,128)} %perm.1, f32[8,2048]{1,0:T(8,128)} %scale.1, bf16[1024,256]{1,0:T(8,128)(2,1)} %feat.1), custom_call_target="tpu_custom_call" | custom-call | tf_op jit(solution)/shard_map/simrank/pallas_call | solution.py:350
  266.8 0.0 copy-start
  266.8 4.7 %copy.9 = bf16[2048,1024]{1,0:T(8,128)(2,1)} copy(bf16[2048,1024]{1,0:T(8,128)(2,1)} %get-tuple-element.4) | data formatting | bytes 8388608
  271.5 0.0 copy-done
  271.5 0.7 copy.10
Async XLA Ops:
  266.8 4.7 %copy-start = (f32[128,256]{1,0:T(8,128)S(1)}, f32[128,256]{1,0:T(8,128)}, u32[]{:S(2)}) copy-start(f32[128,256]{1,0:T(8,128)} %get-tuple-element.5) | copy-start | bytes 393220

commit v2 on v1

--- a/solution.py
+++ b/solution.py
@@ -13,18 +13,28 @@
 F = 256
 CH = 256
 NCH = NB // CH
-PIECE = 128
+PIECE = 256
+NSUB = 4
+SUB = PIECE // NSUB
+AHEAD = 3
+LAG = 2
+HOME_AT = (0, 1)
+PASS_AT = ((), (), (0, 1), (2, 3), (4, 5), (6, 7), (), ())
+TAKE_AT = ((), (), (), (0, 1), (2, 3), (4, 5), (6, 7), ())
+AFTER_PASS = ((), ())
+AFTER_TAKE = ((), ())
+AFTER_CROSS = (tuple(range(16)), ())
 BF16 = jnp.bfloat16
 F32 = jnp.float32
 
 
 def kernel(
     sim, diag, perm, scale, feat,
-    new_sim, agg,
+    new_sim, agg, relay,
     s_own, s_par, b_own, onehot, mixed, sent, marr, bt, acc, feats,
     mine_t, perm_row, scale_row, perm_col, inv_scale, part, slots, total,
     load_sem, own_sem,
-    sx, rx, sz, rz, sd, rd, sf, rf, sb, rb, se, sc, rc, sa, ra, out_sem, agg_sem,
+    sx, rx, sz, rz, sd, rd, sf, rf, sb, rb, sq, rq, sy, ry, sc, rc, sa, ra, out_sem, agg_sem,
 ):
     row = lax.axis_index("row")
     col = lax.axis_index("col")
@@ -34,23 +44,15 @@
     sibling = (row, col + 1 - 2 * core)
     x_partner = (row, (col + 8) % 16)
     z_partner = ((row + 4) % 8, col)
-    near = (row, col + 2 - 4 * zl)
-    hold_same = (x // 2 == zh).astype(jnp.int32)
-    hold_piece = y + 4 * (1 - hold_same)
-    hold_zl = lax.rem(zl + 1 - hold_same, 2)
-    parity = y % 2
-    match = (parity == zl).astype(jnp.int32)
-    first = 4 * (1 - match)
-    source_zh = lax.rem(zh + 1 - match, 2)
-
-    def hold_target(i):
-        return block, i * 4 + hold_zl * 2 + core
-
-    def hold_source(i):
-        return source_zh * 4 + i, (row // 2) * 4 + parity * 2 + core
-
-    def is_me(device):
-        return jnp.logical_and(device[0] == row, device[1] == col)
+    z_near = (row, col + 2 - 4 * zl)
+    z_mirror = ((1 - zh) * 4 + y, x * 4 + (1 - zl) * 2 + core)
+    x_pair = (row, col + 4 - 8 * (x % 2))
+    x_other = (row, (col + 12 + 8 * (x % 2)) % 16)
+    home = x // 2 == zh
+    home_int = home.astype(jnp.int32)
+    pair = 2 * lax.rem(x + 1 - home_int, 2)
+    order = (pair + zl, pair + 1 - zl, 2 - pair + zl, 3 - pair - zl)
+    held = 2 * (x % 2) + zl
 
     barrier = pltpu.get_barrier_semaphore()
 
@@ -59,18 +61,10 @@
 
     for i in range(1, 16):
         greet((row, (col + i) % 16))
+    for i in range(1, 4):
+        greet((zh * 4 + (y + i) % 4, col))
     greet(z_partner)
-    own_source = jnp.int32(0)
-    for i in range(4):
-        device = hold_source(i)
-
-        @pl.when(jnp.logical_not(is_me(device)))
-        def _():
-            greet(device)
-
-    out_count = jnp.int32(16)
-    for i in range(4):
-        out_count = out_count + jnp.where(is_me(hold_target(i)), 0, 1)
+    greet(z_mirror)
 
     loads = [
         pltpu.make_async_copy(diag, b_own, load_sem.at[0]),
@@ -87,7 +81,7 @@
 
     for i in range(NCH):
         own_load(i).start()
-    pl.semaphore_wait(barrier, out_count)
+    pl.semaphore_wait(barrier, 20)
 
     def remote(src, dst, send, recv, device):
         return pltpu.make_async_remote_copy(
@@ -119,52 +113,117 @@
         rows = pl.ds(i * CH, CH)
         return remote(sent.at[rows], marr.at[rows], sz.at[i], rz.at[i], z_partner)
 
-    def bt_rows(half, piece):
-        return pl.ds(pl.multiple_of(half * HALF + piece * PIECE, PIECE), PIECE)
-
-    def piece_copy(i):
-        device = hold_target(i)
+    def bt_rows(half, part_of):
+        return bt.at[pl.ds(pl.multiple_of(half * HALF + part_of * PIECE, PIECE), PIECE)]
+
+    def near_half():
+        rows = pl.ds(0, PIECE // 2)
         return remote(
-            mine_t, bt.at[bt_rows(core, hold_piece)], sb.at[i], rb.at[hold_piece], device
-        )
-
-    def piece_arrival(q):
-        return remote(mine_t, bt.at[bt_rows(core, q)], sb.at[0], rb.at[q], near)
-
-    def near_copy(i):
-        rows = bt_rows(core, first + i)
-        return remote(bt.at[rows], bt.at[rows], se.at[i], rb.at[first + i], near)
-
-    def core_copy(q):
-        rows = bt_rows(core, q)
-        return remote(bt.at[rows], bt.at[rows], sc.at[q], rc.at[q], sibling)
-
-    def core_arrival(q):
-        return remote(mine_t, bt.at[bt_rows(1 - core, q)], sc.at[q], rc.at[q], sibling)
-
-    for i in range(2):
+            mine_t.at[rows], relay.at[held, rows], sb.at[0], rb.at[0], z_near
+        )
+
+    def mirror_half():
+        rows = pl.ds(PIECE // 2, PIECE // 2)
+        return remote(
+            mine_t.at[rows], relay.at[held, rows], sb.at[1], rb.at[1], z_mirror
+        )
+
+    def held_copy(n):
+        rows = pl.ds(n * SUB, SUB)
+        return pltpu.make_async_copy(mine_t.at[rows], relay.at[held, rows], rq.at[held, n])
+
+    def sub(n):
+        return pl.ds(n * SUB, SUB)
+
+    def along_x(k, n, where):
+        device = (x_pair, x_other)[where]
+        source = order[k]
+        return remote(
+            relay.at[source, sub(n)], relay.at[source, sub(n)],
+            sq.at[k % 2, where, n], rq.at[source, n], device,
+        )
+
+    def bt_sub(half, u, n):
+        start = pl.multiple_of(half * HALF + u * PIECE + n * SUB, SUB)
+        return bt.at[pl.ds(start, SUB)]
+
+    def along_y(target, n):
+        return remote(
+            relay.at[target, sub(n)], bt_sub(core, y, n),
+            sy.at[target, n], ry.at[y, n], (zh * 4 + target, col),
+        )
+
+    def stay(n):
+        return pltpu.make_async_copy(relay.at[y, sub(n)], bt_sub(core, y, n), ry.at[y, n])
+
+    def y_arrival(u, n):
+        return remote(mine_t.at[sub(n)], bt_sub(core, u, n), sy.at[u, n], ry.at[u, n], sibling)
+
+    def core_copy(u, n):
+        return remote(
+            bt_sub(core, u, n), bt_sub(core, u, n), sc.at[u, n], rc.at[u, n], sibling
+        )
+
+    def core_arrival(u, n):
+        return remote(
+            mine_t.at[sub(n)], bt_sub(1 - core, u, n), sc.at[u, n], rc.at[u, n], sibling
+        )
+
+    def give_y(target, n):
+        @pl.when(target != y)
+        def _():
+            along_y(target, n).start()
+
+        @pl.when(target == y)
+        def _():
+            stay(n).start()
+
+    def hand_out(k):
+        for n in range(NSUB):
+            along_x(k, n, 0).start()
+            along_x(k, n, 1).start()
+        for n in range(NSUB):
+            give_y(order[k], n)
+
+    def pass_on(m):
+        k, n = m // NSUB, m % NSUB
+
+        @pl.when(jnp.logical_not(home))
+        def _():
+            along_x(k, n, 0).wait_recv()
+            along_x(k, n, 0).start()
+            give_y(order[k], n)
+
+    def take_in(m):
+        k, n = 2 + m // NSUB, m % NSUB
+        along_x(k, n, 0).wait_recv()
+        give_y(order[k], n)
+
+    def cross(m):
+        u, n = m // NSUB, m % NSUB
+        y_arrival(u, n).wait_recv()
+        core_copy(u, n).start()
+
+    for i in range(AHEAD):
         x_copy(i).start()
     for i in range(NCH):
         own_copy(i).start()
 
     loads[0].wait()
-    piece_cols = pl.ds(pl.multiple_of(hold_piece * PIECE, PIECE), PIECE)
+    piece_cols = pl.ds(pl.multiple_of(y * PIECE, PIECE), PIECE)
     for i in range(NB // PIECE):
         rows = pl.ds(i * PIECE, PIECE)
         mine_t[:, rows] = b_own[rows, piece_cols].astype(F32).T.astype(BF16)
-    for i in range(4):
-        device = hold_target(i)
-        self_copy = is_me(device)
-
-        @pl.when(jnp.logical_not(self_copy))
-        def _():
-            piece_copy(i).start()
-
-        @pl.when(self_copy)
-        def _():
-            pltpu.make_async_copy(
-                mine_t, bt.at[bt_rows(core, hold_piece)], rb.at[hold_piece]
-            ).start()
+
+    @pl.when(home)
+    def _():
+        near_half().start()
+        for n in range(NSUB):
+            held_copy(n).start()
+
+    @pl.when(jnp.logical_not(home))
+    def _():
+        mirror_half().start()
 
     col_source = (block + 4) % 8
     row_source = (row + 4) % 8
@@ -199,22 +258,40 @@
         hit = jnp.where(here == perm_row[2:3, :], scale_row[1:2, :], 0.0)
         inv_scale[rows, :] = jnp.broadcast_to(jnp.sum(hit, axis=1, keepdims=True), (128, 128))
 
+    def gathered(rows, i):
+        wanted = perm_col[rows, :]
+        wanted = jnp.concatenate([wanted, wanted], axis=1)
+        here = lax.broadcasted_iota(jnp.int32, (CH, CH), 1) + i * CH
+        pick = jnp.where(here == wanted, 1.0, 0.0).astype(BF16)
+        far = marr[pl.ds(pl.multiple_of(i * CH, CH), CH), :]
+        return jnp.dot(pick, far, preferred_element_type=F32)
+
+    def add_matched(i):
+        z_copy(i).wait_recv()
+
+        @pl.loop(0, NCH)
+        def _(t):
+            rows = pl.ds(pl.multiple_of(t * CH, CH), CH)
+            far = gathered(rows, i)
+
+            @pl.when(i == 0)
+            def _():
+                acc[rows, :] = far
+
+            @pl.when(i > 0)
+            def _():
+                acc[rows, :] += far
+
     @pl.loop(0, NCH)
     def _(i):
         rows = pl.ds(pl.multiple_of(i * CH, CH), CH)
 
-        @pl.when(i + 2 < NCH)
-        def _():
-            x_copy(i + 2).start()
+        @pl.when(i + AHEAD < NCH)
+        def _():
+            x_copy(i + AHEAD).start()
 
         x_copy(i).wait_recv()
         forward(i).start()
-
-        @pl.when(jnp.logical_and(i >= 2, i < 6))
-        def _():
-            piece_arrival(first + i - 2).wait_recv()
-            near_copy(i - 2).start()
-            core_copy(first + i - 2).start()
 
         own_load(i).wait()
         own_arrival(i).wait_recv()
@@ -238,50 +315,46 @@
 
         z_copy(i).start()
 
-    other = 4 - first
-
-    @pl.loop(0, 4)
-    def _(i):
-        piece_arrival(other + i).wait_recv()
-        core_copy(other + i).start()
-
-    @pl.loop(0, 8)
-    def _(q):
-        core_arrival(q).wait_recv()
-
-    @pl.loop(0, NCH)
-    def _(t):
-        rows = pl.ds(pl.multiple_of(t * CH, CH), CH)
-
-        @pl.loop(0, HALF // 512)
-        def _(n):
-            cols = pl.ds(pl.multiple_of(n * 512, 512), 512)
-            acc[rows, cols] = jnp.dot(bt[rows, :], mixed[:, cols], preferred_element_type=F32)
-
-    def gathered(rows, i, cols):
-        wanted = perm_col[rows, :]
-        wanted = jnp.concatenate([wanted, wanted], axis=1)
-        here = lax.broadcasted_iota(jnp.int32, (CH, CH), 1) + i * CH
-        pick = jnp.where(here == wanted, 1.0, 0.0).astype(BF16)
-        far = marr[pl.ds(pl.multiple_of(i * CH, CH), CH), cols]
-        return jnp.dot(pick, far, preferred_element_type=F32)
-
-    @pl.loop(0, NCH - 1)
-    def _(i):
-        z_copy(i).wait_recv()
-
-        @pl.loop(0, NCH)
-        def _(t):
-            rows = pl.ds(pl.multiple_of(t * CH, CH), CH)
-            acc[rows, :] += gathered(rows, i, pl.ds(0, HALF))
-
-    z_copy(NCH - 1).wait_recv()
+        @pl.when(jnp.logical_and(home, i == HOME_AT[0]))
+        def _():
+            for n in range(NSUB):
+                held_copy(n).wait()
+            hand_out(0)
+
+        @pl.when(jnp.logical_and(home, i == HOME_AT[1]))
+        def _():
+            near_half().wait_recv()
+            mirror_half().wait_recv()
+            hand_out(1)
+
+        for step in range(NCH):
+            if PASS_AT[step] or TAKE_AT[step]:
+                @pl.when(i == step)
+                def _():
+                    for m in PASS_AT[step]:
+                        pass_on(m)
+                    for m in TAKE_AT[step]:
+                        take_in(m)
+
+        @pl.when(i >= LAG)
+        def _():
+            add_matched(i - LAG)
+
+    for i in range(NCH - LAG, NCH):
+        for m in AFTER_PASS[i - NCH + LAG]:
+            pass_on(m)
+        for m in AFTER_TAKE[i - NCH + LAG]:
+            take_in(m)
+        for m in AFTER_CROSS[i - NCH + LAG]:
+            cross(m)
+        add_matched(i)
+
     loads[1].wait()
     offset = col * HALF - row * NB
 
     def out_copy(t):
         rows = pl.ds(pl.multiple_of(t * CH, CH), CH)
-        return pltpu.make_async_copy(mixed.at[rows], new_sim.at[rows], out_sem.at[t])
+        return pltpu.make_async_copy(sent.at[rows], new_sim.at[rows], out_sem.at[t])
 
     def part_copy(owner):
         rows = pl.ds(pl.multiple_of(owner * 128, 128), 128)
@@ -291,13 +364,27 @@
         return remote(part.at[pl.ds(0, 128)], slots.at[i], sa.at[i], ra.at[i], sibling)
 
     @pl.loop(0, NCH)
-    def _(t):
+    def _(i):
+        z_copy(i).wait_send()
+
+    @pl.loop(0, NCH)
+    def _(step):
+        u = step // 2
+        half = lax.rem(step + core, 2)
+        t = half * (NCH // 2) + u
         rows = pl.ds(pl.multiple_of(t * CH, CH), CH)
-        value = decay_factor * (acc[rows, :] + gathered(rows, NCH - 1, pl.ds(0, HALF)))
+
+        @pl.when(half != core)
+        def _():
+            for n in range(NSUB):
+                core_arrival(u, n).wait_recv()
+
+        value = acc[rows, :] + jnp.dot(bt[rows, :], mixed[...], preferred_element_type=F32)
+        value = decay_factor * value
         down = lax.broadcasted_iota(jnp.int32, (CH, HALF), 0) + t * CH
         across = lax.broadcasted_iota(jnp.int32, (CH, HALF), 1) + offset
         value = jnp.where(down == across, 1.0, value).astype(BF16)
-        mixed[rows, :] = value
+        sent[rows, :] = value
         out_copy(t).start()
         part[rows, :] = jnp.dot(value, feats[...], preferred_element_type=F32).astype(BF16)
         for k in range(2):
@@ -325,16 +412,30 @@
         x_copy(i).wait_send()
         own_copy(i).wait_send()
         forward(i).wait_send()
-        z_copy(i).wait_send()
-        core_copy(i).wait_send()
         out_copy(i).wait()
 
-    for i in range(4):
-        near_copy(i).wait_send()
-
-        @pl.when(jnp.logical_not(is_me(hold_target(i))))
-        def _():
-            piece_copy(i).wait_send()
+    for n in range(NSUB):
+        for u in range(4):
+            core_copy(u, n).wait_send()
+
+            @pl.when(u != y)
+            def _():
+                along_y(u, n).wait_send()
+
+        for k in range(2):
+            along_x(k, n, 0).wait_send()
+
+            @pl.when(home)
+            def _():
+                along_x(k, n, 1).wait_send()
+
+    @pl.when(home)
+    def _():
+        near_half().wait_send()
+
+    @pl.when(jnp.logical_not(home))
+    def _():
+        mirror_half().wait_send()
 
     @pl.loop(0, 16)
     def _(i):
@@ -352,6 +453,7 @@
         out_shape=(
             jax.ShapeDtypeStruct((NB, HALF), BF16),
             jax.ShapeDtypeStruct((128, F), F32),
+            jax.ShapeDtypeStruct((4, PIECE, NB), BF16),
         ),
         in_specs=[
             pl.BlockSpec(memory_space=pl.ANY),
@@ -361,6 +463,7 @@
             pl.BlockSpec(memory_space=pl.ANY),
         ],
         out_specs=(
+            pl.BlockSpec(memory_space=pl.ANY),
             pl.BlockSpec(memory_space=pl.ANY),
             pl.BlockSpec(memory_space=pl.ANY),
         ),
@@ -388,8 +491,10 @@
             dma((NCH,)), dma((NCH,)),
             dma((NCH,)), dma((NCH,)),
             dma((NCH,)), dma((NCH,)),
-            dma((4,)), dma((8,)), dma((4,)),
-            dma((8,)), dma((8,)),
+            dma((2,)), dma((2,)),
+            dma((2, 2, NSUB)), dma((4, NSUB)),
+            dma((4, NSUB)), dma((4, NSUB)),
+            dma((4, NSUB)), dma((4, NSUB)),
             dma((16,)), dma((16,)),
             dma((NCH,)), dma(()),
         ],
@@ -397,7 +502,7 @@
             collective_id=0, has_side_effects=True, vmem_limit_bytes=60 * 2**20
         ),
         name="simrank",
-    )(sim, diag_blocks, match_perm, match_scale, features)
+    )(sim, diag_blocks, match_perm, match_scale, features)[:2]
 
 
 def solution(mesh):

time: 272 us -> 203 us (0.75)
  Pallas kernels: 266 us -> 196 us
    pallas_call x1, Pallas kernels: 266 us -> 196 us  [on_device(): pl.pallas_call(kernel, out_shape=(jax.ShapeDtypeStruct((NB, HALF), BF16),...]
where the time goes in v2:
time: 203 us; the launch traced here: 202 us
  Pallas kernels  196 us (97%)
  local copies, waits for them, and re-layouts  5.34 us (3%)
    pallas_call x1, Pallas kernels, on_device(): pl.pallas_call(kernel, out_shape=(jax.ShapeDtypeStruct((NB, HALF), BF16),...  196 us
    unnamed x4, local copies, waits for them, and re-layouts  5.34 us

profile of v2, /device:TPU:39, one launch (start us, length us, event | category | flops | bytes accessed | tf_op | source)
XLA Modules:
  0.0 202.3 jit_solution(4081953812792057620)
XLA Ops:
  0.6 196.3 %simrank.1 = (bf16[2048,1024]{1,0:T(8,128)(2,1)}, f32[128,256]{1,0:T(8,128)}, bf16[4,256,2048]{2,1,0:T(8,128)(2,1)}) custom-call(bf16[2048,1024]{1,0:T(8,128)(2,1)} %sim.1, bf16[2048,1024]{1,0:T(8,128)(2,1)} %diag.1, s32[8,2048]{1,0:T(8,128)} %perm.1, f32[8,2048]{1,0:T(8,128)} %scale.1, bf16[1024,256]{1,0:T(8,128)(2,1)} %feat.1), custom_call_target="tpu_custom_call" | custom-call | tf_op jit(solution)/shard_map/simrank/pallas_call | solution.py:451
  197.0 0.0 copy-start
  197.0 4.7 %copy.9 = bf16[2048,1024]{1,0:T(8,128)(2,1)} copy(bf16[2048,1024]{1,0:T(8,128)(2,1)} %get-tuple-element.8) | data formatting | bytes 8388608
  201.7 0.0 copy-done
  201.7 0.7 copy.10
Async XLA Ops:
  197.0 4.7 %copy-start = (f32[128,256]{1,0:T(8,128)S(1)}, f32[128,256]{1,0:T(8,128)}, u32[]{:S(2)}) copy-start(f32[128,256]{1,0:T(8,128)} %get-tuple-element.9) | copy-start | bytes 393220

commit v3 on v2

--- a/solution.py
+++ b/solution.py
@@ -15,15 +15,14 @@
 NCH = NB // CH
 PIECE = 256
 NSUB = 4
+OVER_Z = 2
 SUB = PIECE // NSUB
-AHEAD = 3
+AHEAD = 2
 LAG = 2
-HOME_AT = (0, 1)
-PASS_AT = ((), (), (0, 1), (2, 3), (4, 5), (6, 7), (), ())
-TAKE_AT = ((), (), (), (0, 1), (2, 3), (4, 5), (6, 7), ())
-AFTER_PASS = ((), ())
-AFTER_TAKE = ((), ())
-AFTER_CROSS = (tuple(range(16)), ())
+PASS_AT = ((0, 1), (2, 3), (4, 5), (6, 7), (), (), (), ())
+TAKE_AT = ((0,), (1, 2), (3, 4), (5, 6), (7,), (), (), ())
+AFTER_PASS = ()
+AFTER_TAKE = ()
 BF16 = jnp.bfloat16
 F32 = jnp.float32
 
@@ -34,7 +33,7 @@
     s_own, s_par, b_own, onehot, mixed, sent, marr, bt, acc, feats,
     mine_t, perm_row, scale_row, perm_col, inv_scale, part, slots, total,
     load_sem, own_sem,
-    sx, rx, sz, rz, sd, rd, sf, rf, sb, rb, sq, rq, sy, ry, sc, rc, sa, ra, out_sem, agg_sem,
+    sx, rx, sz, rz, sd, rd, sf, rf, sb, rb, sq, rq, sv, sy, ry, sc, rc, sp, rp, sa, ra, out_sem, agg_sem,
 ):
     row = lax.axis_index("row")
     col = lax.axis_index("col")
@@ -178,8 +177,15 @@
         def _():
             stay(n).start()
 
+    def over_z(k, n):
+        source = order[k]
+        return remote(
+            relay.at[source, sub(n)], relay.at[source, sub(n)],
+            sv.at[k // 2, n], rq.at[source, n], z_near,
+        )
+
     def hand_out(k):
-        for n in range(NSUB):
+        for n in range(NSUB if k == 0 else OVER_Z):
             along_x(k, n, 0).start()
             along_x(k, n, 1).start()
         for n in range(NSUB):
@@ -191,12 +197,17 @@
         @pl.when(jnp.logical_not(home))
         def _():
             along_x(k, n, 0).wait_recv()
-            along_x(k, n, 0).start()
+            if k == 0 or n < OVER_Z:
+                along_x(k, n, 0).start()
+            if k == 0 and n >= OVER_Z:
+                over_z(k, n).start()
             give_y(order[k], n)
 
     def take_in(m):
         k, n = 2 + m // NSUB, m % NSUB
         along_x(k, n, 0).wait_recv()
+        if k == 2 and n >= OVER_Z:
+            over_z(k, n).start()
         give_y(order[k], n)
 
     def cross(m):
@@ -220,6 +231,9 @@
         near_half().start()
         for n in range(NSUB):
             held_copy(n).start()
+        for n in range(NSUB):
+            held_copy(n).wait()
+        hand_out(0)
 
     @pl.when(jnp.logical_not(home))
     def _():
@@ -253,10 +267,13 @@
 
     @pl.loop(0, NB // 128)
     def _(i):
-        rows = pl.ds(i * 128, 128)
         here = lax.broadcasted_iota(jnp.int32, (128, NB), 0) + i * 128
         hit = jnp.where(here == perm_row[2:3, :], scale_row[1:2, :], 0.0)
-        inv_scale[rows, :] = jnp.broadcast_to(jnp.sum(hit, axis=1, keepdims=True), (128, 128))
+        place = pl.ds(pl.multiple_of((i % 8) * 128, 128), 128)
+        lanes = pl.ds(pl.multiple_of((i // 8) * 128, 128), 128)
+        inv_scale[place, lanes] = jnp.broadcast_to(
+            jnp.sum(hit, axis=1, keepdims=True), (128, 128)
+        )
 
     def gathered(rows, i):
         wanted = perm_col[rows, :]
@@ -281,6 +298,12 @@
             @pl.when(i > 0)
             def _():
                 acc[rows, :] += far
+
+    @pl.when(home)
+    def _():
+        near_half().wait_recv()
+        mirror_half().wait_recv()
+        hand_out(1)
 
     @pl.loop(0, NCH)
     def _(i):
@@ -308,24 +331,15 @@
             value += moved * scale_row[0:1, here]
             value = value.astype(BF16)
             mixed[rows, cols] = value
-            lanes = inv_scale[rows, :]
+            lanes = inv_scale[
+                pl.ds(pl.multiple_of((i % 4) * CH, CH), CH),
+                pl.ds(pl.multiple_of((i // 4) * 128, 128), 128),
+            ]
             sent[rows, cols] = (
                 value.astype(F32) * jnp.concatenate([lanes, lanes], axis=1)
             ).astype(BF16)
 
         z_copy(i).start()
-
-        @pl.when(jnp.logical_and(home, i == HOME_AT[0]))
-        def _():
-            for n in range(NSUB):
-                held_copy(n).wait()
-            hand_out(0)
-
-        @pl.when(jnp.logical_and(home, i == HOME_AT[1]))
-        def _():
-            near_half().wait_recv()
-            mirror_half().wait_recv()
-            hand_out(1)
 
         for step in range(NCH):
             if PASS_AT[step] or TAKE_AT[step]:
@@ -340,69 +354,98 @@
         def _():
             add_matched(i - LAG)
 
-    for i in range(NCH - LAG, NCH):
-        for m in AFTER_PASS[i - NCH + LAG]:
-            pass_on(m)
-        for m in AFTER_TAKE[i - NCH + LAG]:
-            take_in(m)
-        for m in AFTER_CROSS[i - NCH + LAG]:
-            cross(m)
-        add_matched(i)
-
-    loads[1].wait()
-    offset = col * HALF - row * NB
-
-    def out_copy(t):
-        rows = pl.ds(pl.multiple_of(t * CH, CH), CH)
-        return pltpu.make_async_copy(sent.at[rows], new_sim.at[rows], out_sem.at[t])
-
-    def part_copy(owner):
-        rows = pl.ds(pl.multiple_of(owner * 128, 128), 128)
-        return remote(part.at[rows], slots.at[col], sa.at[owner], ra.at[col], (row, owner))
-
-    def part_arrival(i):
-        return remote(part.at[pl.ds(0, 128)], slots.at[i], sa.at[i], ra.at[i], sibling)
-
-    @pl.loop(0, NCH)
-    def _(i):
-        z_copy(i).wait_send()
+    for m in AFTER_PASS:
+        pass_on(m)
+    for m in AFTER_TAKE:
+        take_in(m)
+    for m in range(4 * NSUB):
+        cross(m)
 
     @pl.loop(0, NCH)
     def _(step):
         u = step // 2
         half = lax.rem(step + core, 2)
-        t = half * (NCH // 2) + u
-        rows = pl.ds(pl.multiple_of(t * CH, CH), CH)
+        rows = pl.ds(pl.multiple_of((half * (NCH // 2) + u) * CH, CH), CH)
 
         @pl.when(half != core)
         def _():
             for n in range(NSUB):
                 core_arrival(u, n).wait_recv()
 
-        value = acc[rows, :] + jnp.dot(bt[rows, :], mixed[...], preferred_element_type=F32)
-        value = decay_factor * value
+        @pl.loop(0, HALF // 512)
+        def _(n):
+            cols = pl.ds(pl.multiple_of(n * 512, 512), 512)
+            acc[rows, cols] += jnp.dot(bt[rows, :], mixed[:, cols], preferred_element_type=F32)
+
+    for i in range(NCH - LAG, NCH - 1):
+        add_matched(i)
+    z_copy(NCH - 1).wait_recv()
+
+    loads[1].wait()
+    offset = col * HALF - row * NB
+
+    def out_copy(t):
+        rows = pl.ds(pl.multiple_of(t * CH, CH), CH)
+        return pltpu.make_async_copy(sent.at[rows], new_sim.at[rows], out_sem.at[t])
+
+    def line_of(t):
+        return pl.ds(pl.multiple_of(t * 128, 128), 128)
+
+    def give_copy(t):
+        rows = pl.ds(pl.multiple_of(t * CH + (1 - core) * 128, 128), 128)
+        return remote(
+            acc.at[rows, pl.ds(0, F)], inv_scale.at[line_of(t)], sp.at[t], rp.at[t], sibling
+        )
+
+    def part_copy(t):
+        device = (row, 2 * t + core)
+        return remote(part.at[line_of(t)], slots.at[block], sa.at[t], ra.at[block], device)
+
+    def part_arrival(i):
+        return remote(part.at[line_of(0)], slots.at[i], sa.at[i], ra.at[i], sibling)
+
+    def settle(t):
+        give_copy(t).wait_recv()
+        rows = pl.ds(pl.multiple_of(t * CH + core * 128, 128), 128)
+        kept = acc[rows, pl.ds(0, F)] + inv_scale[line_of(t), :]
+
+        @pl.when(t != block)
+        def _():
+            part[line_of(t), :] = kept.astype(BF16)
+            part_copy(t).start()
+
+        @pl.when(t == block)
+        def _():
+            total[...] = kept
+
+    @pl.loop(0, NCH)
+    def _(i):
+        z_copy(i).wait_send()
+
+    @pl.loop(0, NCH)
+    def _(step):
+        t = (step + block + 1) % NCH
+        rows = pl.ds(pl.multiple_of(t * CH, CH), CH)
+        value = decay_factor * (acc[rows, :] + gathered(rows, NCH - 1))
         down = lax.broadcasted_iota(jnp.int32, (CH, HALF), 0) + t * CH
         across = lax.broadcasted_iota(jnp.int32, (CH, HALF), 1) + offset
         value = jnp.where(down == across, 1.0, value).astype(BF16)
         sent[rows, :] = value
         out_copy(t).start()
-        part[rows, :] = jnp.dot(value, feats[...], preferred_element_type=F32).astype(BF16)
-        for k in range(2):
-            owner = 2 * t + k
-
-            @pl.when(owner != col)
-            def _():
-                part_copy(owner).start()
-
-    mine = part[pl.ds(pl.multiple_of(col * 128, 128), 128), :].astype(F32)
-    total[...] = mine
-
-    @pl.loop(0, 16)
+        acc[rows, pl.ds(0, F)] = jnp.dot(value, feats[...], preferred_element_type=F32)
+        give_copy(t).start()
+
+        @pl.when(step > 0)
+        def _():
+            settle((step + block) % NCH)
+
+    settle(block)
+
+    @pl.loop(1, NCH)
     def _(i):
-        @pl.when(i != col)
-        def _():
-            part_arrival(i).wait_recv()
-            total[...] += slots[i].astype(F32)
+        source = (block + NCH - i) % NCH
+        part_arrival(source).wait_recv()
+        total[...] += slots[source].astype(F32)
 
     agg_copy = pltpu.make_async_copy(total, agg, agg_sem)
     agg_copy.start()
@@ -422,12 +465,20 @@
             def _():
                 along_y(u, n).wait_send()
 
+        if n >= OVER_Z:
+            over_z(2, n).wait_send()
+
+            @pl.when(jnp.logical_not(home))
+            def _():
+                over_z(0, n).wait_send()
+
         for k in range(2):
-            along_x(k, n, 0).wait_send()
-
-            @pl.when(home)
-            def _():
-                along_x(k, n, 1).wait_send()
+            if k == 0 or n < OVER_Z:
+                along_x(k, n, 0).wait_send()
+
+                @pl.when(home)
+                def _():
+                    along_x(k, n, 1).wait_send()
 
     @pl.when(home)
     def _():
@@ -437,11 +488,13 @@
     def _():
         mirror_half().wait_send()
 
-    @pl.loop(0, 16)
-    def _(i):
-        @pl.when(i != col)
-        def _():
-            part_copy(i).wait_send()
+    @pl.loop(0, NCH)
+    def _(t):
+        give_copy(t).wait_send()
+
+        @pl.when(t != block)
+        def _():
+            part_copy(t).wait_send()
 
     agg_copy.wait()
 
@@ -482,9 +535,9 @@
             pltpu.VMEM((8, NB), jnp.int32),
             pltpu.VMEM((8, NB), F32),
             pltpu.VMEM((NB, 128), jnp.int32),
-            pltpu.VMEM((NB, 128), F32),
-            pltpu.VMEM((NB, F), BF16),
-            pltpu.VMEM((16, 128, F), BF16),
+            pltpu.VMEM((HALF, 256), F32),
+            pltpu.VMEM((HALF, F), BF16),
+            pltpu.VMEM((8, 128, F), BF16),
             pltpu.VMEM((128, F), F32),
             dma((2,)), dma((NCH,)),
             dma((NCH,)), dma((NCH,)),
@@ -492,10 +545,11 @@
             dma((NCH,)), dma((NCH,)),
             dma((NCH,)), dma((NCH,)),
             dma((2,)), dma((2,)),
-            dma((2, 2, NSUB)), dma((4, NSUB)),
+            dma((2, 2, NSUB)), dma((4, NSUB)), dma((2, NSUB)),
             dma((4, NSUB)), dma((4, NSUB)),
             dma((4, NSUB)), dma((4, NSUB)),
-            dma((16,)), dma((16,)),
+            dma((8,)), dma((8,)),
+            dma((8,)), dma((8,)),
             dma((NCH,)), dma(()),
         ],
         compiler_params=pltpu.CompilerParams(

time: 203 us -> 180 us (0.89)
  Pallas kernels: 196 us -> 174 us
    pallas_call x1, Pallas kernels: 196 us -> 174 us  [on_device(): pl.pallas_call(kernel, out_shape=(jax.ShapeDtypeStruct((NB, HALF), BF16),...]
where the time goes in v3:
time: 180 us
  Pallas kernels  174 us (97%)
  local copies, waits for them, and re-layouts  5.34 us (3%)
    pallas_call x1, Pallas kernels, on_device(): pl.pallas_call(kernel, out_shape=(jax.ShapeDtypeStruct((NB, HALF), BF16),...  174 us
    unnamed x4, local copies, waits for them, and re-layouts  5.34 us

profile of v3, /device:TPU:39, one launch (start us, length us, event | category | flops | bytes accessed | tf_op | source)
XLA Modules:
  0.0 179.6 jit_solution(7274214950542333859)
XLA Ops:
  0.6 173.6 %simrank.1 = (bf16[2048,1024]{1,0:T(8,128)(2,1)}, f32[128,256]{1,0:T(8,128)}, bf16[4,256,2048]{2,1,0:T(8,128)(2,1)}) custom-call(bf16[2048,1024]{1,0:T(8,128)(2,1)} %sim.1, bf16[2048,1024]{1,0:T(8,128)(2,1)} %diag.1, s32[8,2048]{1,0:T(8,128)} %perm.1, f32[8,2048]{1,0:T(8,128)} %scale.1, bf16[1024,256]{1,0:T(8,128)(2,1)} %feat.1), custom_call_target="tpu_custom_call" | custom-call | tf_op jit(solution)/shard_map/simrank/pallas_call | solution.py:504
  174.3 0.0 copy-start
  174.3 4.7 %copy.9 = bf16[2048,1024]{1,0:T(8,128)(2,1)} copy(bf16[2048,1024]{1,0:T(8,128)(2,1)} %get-tuple-element.8) | data formatting | bytes 8388608
  178.9 0.0 copy-done
  178.9 0.7 copy.10
Async XLA Ops:
  174.3 4.7 %copy-start = (f32[128,256]{1,0:T(8,128)S(1)}, f32[128,256]{1,0:T(8,128)}, u32[]{:S(2)}) copy-start(f32[128,256]{1,0:T(8,128)} %get-tuple-element.9) | copy-start | bytes 393220

commit v4 on v3

--- a/solution.py
+++ b/solution.py
@@ -19,8 +19,8 @@
 SUB = PIECE // NSUB
 AHEAD = 2
 LAG = 2
-PASS_AT = ((0, 1), (2, 3), (4, 5), (6, 7), (), (), (), ())
-TAKE_AT = ((0,), (1, 2), (3, 4), (5, 6), (7,), (), (), ())
+PASS_AT = ((0, 1, 2, 3), (4, 5, 6, 7), (), (), (), (), (), ())
+TAKE_AT = ((0, 1), (2, 3, 4), (5, 6, 7), (), (), (), (), ())
 AFTER_PASS = ()
 AFTER_TAKE = ()
 BF16 = jnp.bfloat16
@@ -499,9 +499,24 @@
     agg_copy.wait()
 
 
+def finish(made, summed, new_sim, agg, held, held_sum, into, out):
+    rows = [pl.ds(i * (NB // 4), NB // 4) for i in range(4)]
+    reads = [pltpu.make_async_copy(made.at[r], held.at[r], into.at[i]) for i, r in enumerate(rows)]
+    reads.append(pltpu.make_async_copy(summed, held_sum, into.at[4]))
+    writes = [pltpu.make_async_copy(held.at[r], new_sim.at[r], out.at[i]) for i, r in enumerate(rows)]
+    writes.append(pltpu.make_async_copy(held_sum, agg, out.at[4]))
+    for read in reads:
+        read.start()
+    for read, write in zip(reads, writes):
+        read.wait()
+        write.start()
+    for write in writes:
+        write.wait()
+
+
 def on_device(sim, diag_blocks, match_perm, match_scale, features):
     dma = pltpu.SemaphoreType.DMA
-    return pl.pallas_call(
+    made, summed, _ = pl.pallas_call(
         kernel,
         out_shape=(
             jax.ShapeDtypeStruct((NB, HALF), BF16),
@@ -556,7 +571,24 @@
             collective_id=0, has_side_effects=True, vmem_limit_bytes=60 * 2**20
         ),
         name="simrank",
-    )(sim, diag_blocks, match_perm, match_scale, features)[:2]
+    )(sim, diag_blocks, match_perm, match_scale, features)
+    hbm = pl.BlockSpec(memory_space=pl.ANY)
+    return pl.pallas_call(
+        finish,
+        out_shape=(
+            jax.ShapeDtypeStruct((NB, HALF), BF16),
+            jax.ShapeDtypeStruct((128, F), F32),
+        ),
+        in_specs=[hbm, hbm],
+        out_specs=(hbm, hbm),
+        scratch_shapes=[
+            pltpu.VMEM((NB, HALF), BF16),
+            pltpu.VMEM((128, F), F32),
+            dma((5,)),
+            dma((5,)),
+        ],
+        name="finish",
+    )(made, summed)
 
 
 def solution(mesh):

time: 180 us -> 175 us (0.972)
  local copies, waits for them, and re-layouts: 5.34 us -> 0 us
    unnamed x4 -> x0, local copies, waits for them, and re-layouts: 5.34 us -> none
    pallas_call x0 -> x1, Pallas kernels: none -> 3.35 us  [on_device(): pl.pallas_call(finish, out_shape=(jax.ShapeDtypeStruct((NB, HALF), BF16),...]
    pallas_call x1, Pallas kernels: 174 us -> 171 us  [on_device(): pl.pallas_call(kernel, out_shape=(jax.ShapeDtypeStruct((NB, HALF), BF16),...]
where the time goes in v4:
time: 175 us
  Pallas kernels  174 us (99%)
    pallas_call x1, Pallas kernels, on_device(): pl.pallas_call(kernel, out_shape=(jax.ShapeDtypeStruct((NB, HALF), BF16),...  171 us

profile of v4, /device:TPU:39, one launch (start us, length us, event | category | flops | bytes accessed | tf_op | source)
XLA Modules:
  0.0 174.8 jit_solution(7501932471873910216)
XLA Ops:
  0.6 170.8 %simrank.1 = (bf16[2048,1024]{1,0:T(8,128)(2,1)}, f32[128,256]{1,0:T(8,128)}, bf16[4,256,2048]{2,1,0:T(8,128)(2,1)}) custom-call(bf16[2048,1024]{1,0:T(8,128)(2,1)} %sim.1, bf16[2048,1024]{1,0:T(8,128)(2,1)} %diag.1, s32[8,2048]{1,0:T(8,128)} %perm.1, f32[8,2048]{1,0:T(8,128)} %scale.1, bf16[1024,256]{1,0:T(8,128)(2,1)} %feat.1), custom_call_target="tpu_custom_call" | custom-call | tf_op jit(solution)/shard_map/simrank/pallas_call | solution.py:519
  171.5 3.3 %finish.1 = (bf16[2048,1024]{1,0:T(8,128)(2,1)}, f32[128,256]{1,0:T(8,128)}) custom-call(bf16[2048,1024]{1,0:T(8,128)(2,1)} %get-tuple-element.4.made, f32[128,256]{1,0:T(8,128)} %get-tuple-element.5.summed), custom_call_target="tpu_custom_call" | custom-call | tf_op jit(solution)/shard_map/finish/pallas_call | solution.py:576

commit v5 on v4

--- a/solution.py
+++ b/solution.py
@@ -20,7 +20,7 @@
 AHEAD = 2
 LAG = 2
 PASS_AT = ((0, 1, 2, 3), (4, 5, 6, 7), (), (), (), (), (), ())
-TAKE_AT = ((0, 1), (2, 3, 4), (5, 6, 7), (), (), (), (), ())
+TAKE_AT = ((), (0, 1, 2, 3), (4, 5, 6, 7), (), (), (), (), ())
 AFTER_PASS = ()
 AFTER_TAKE = ()
 BF16 = jnp.bfloat16

time: 175 us -> 174 us (level)
  Pallas kernels: 174 us -> 172 us
    pallas_call x1, Pallas kernels: 171 us -> 169 us  [on_device(): pl.pallas_call(kernel, out_shape=(jax.ShapeDtypeStruct((NB, HALF), BF16),...]
where the time goes in v5:
time: 174 us; the launch traced here: 173 us
  Pallas kernels  172 us (99%)
    pallas_call x1, Pallas kernels, on_device(): pl.pallas_call(kernel, out_shape=(jax.ShapeDtypeStruct((NB, HALF), BF16),...  169 us

profile of v5, /device:TPU:39, one launch (start us, length us, event | category | flops | bytes accessed | tf_op | source)
XLA Modules:
  0.0 172.5 jit_solution(9418722422199596046)
XLA Ops:
  0.6 168.5 %simrank.1 = (bf16[2048,1024]{1,0:T(8,128)(2,1)}, f32[128,256]{1,0:T(8,128)}, bf16[4,256,2048]{2,1,0:T(8,128)(2,1)}) custom-call(bf16[2048,1024]{1,0:T(8,128)(2,1)} %sim.1, bf16[2048,1024]{1,0:T(8,128)(2,1)} %diag.1, s32[8,2048]{1,0:T(8,128)} %perm.1, f32[8,2048]{1,0:T(8,128)} %scale.1, bf16[1024,256]{1,0:T(8,128)(2,1)} %feat.1), custom_call_target="tpu_custom_call" | custom-call | tf_op jit(solution)/shard_map/simrank/pallas_call | solution.py:519
  169.2 3.3 %finish.1 = (bf16[2048,1024]{1,0:T(8,128)(2,1)}, f32[128,256]{1,0:T(8,128)}) custom-call(bf16[2048,1024]{1,0:T(8,128)(2,1)} %get-tuple-element.4.made, f32[128,256]{1,0:T(8,128)} %get-tuple-element.5.summed), custom_call_target="tpu_custom_call" | custom-call | tf_op jit(solution)/shard_map/finish/pallas_call | solution.py:576

commit v6 on v5

--- a/solution.py
+++ b/solution.py
@@ -186,8 +186,9 @@
 
     def hand_out(k):
         for n in range(NSUB if k == 0 else OVER_Z):
+            along_x(k, n, 1).start()
+        for n in range(NSUB if k == 0 else OVER_Z):
             along_x(k, n, 0).start()
-            along_x(k, n, 1).start()
         for n in range(NSUB):
             give_y(order[k], n)
 

time: 174 us -> 174 us (level)
  no operation moved by 1% of the time
where the time goes in v6:
time: 174 us; the launch traced here: 173 us
  Pallas kernels  172 us (99%)
    pallas_call x1, Pallas kernels, on_device(): pl.pallas_call(kernel, out_shape=(jax.ShapeDtypeStruct((NB, HALF), BF16),...  169 us

profile of v6, /device:TPU:39, one launch (start us, length us, event | category | flops | bytes accessed | tf_op | source)
XLA Modules:
  0.0 172.5 jit_solution(14213206580600530096)
XLA Ops:
  0.6 168.5 %simrank.1 = (bf16[2048,1024]{1,0:T(8,128)(2,1)}, f32[128,256]{1,0:T(8,128)}, bf16[4,256,2048]{2,1,0:T(8,128)(2,1)}) custom-call(bf16[2048,1024]{1,0:T(8,128)(2,1)} %sim.1, bf16[2048,1024]{1,0:T(8,128)(2,1)} %diag.1, s32[8,2048]{1,0:T(8,128)} %perm.1, f32[8,2048]{1,0:T(8,128)} %scale.1, bf16[1024,256]{1,0:T(8,128)(2,1)} %feat.1), custom_call_target="tpu_custom_call" | custom-call | tf_op jit(solution)/shard_map/simrank/pallas_call | solution.py:520
  169.2 3.3 %finish.1 = (bf16[2048,1024]{1,0:T(8,128)(2,1)}, f32[128,256]{1,0:T(8,128)}) custom-call(bf16[2048,1024]{1,0:T(8,128)(2,1)} %get-tuple-element.4.made, f32[128,256]{1,0:T(8,128)} %get-tuple-element.5.summed), custom_call_target="tpu_custom_call" | custom-call | tf_op jit(solution)/shard_map/finish/pallas_call | solution.py:577
